TPU v7x, 512 devices: a whole 4x4x16 slice. The times are simulated.
512 devices in a mesh: ka: 32 (over x, y, core), hist: 16 (over z).
Axes of the slice: x: 4, y: 4, z: 16, core: 2. Of those that a mesh axis runs over, the one named last changes fastest.
Arguments:
- green_row: float32 [1024, 576, 128], P('hist', 'ka'), may hold values from -6 to 6
- screened: float32 [1024, 576, 128], P('hist', 'ka'), may hold values from -0.2 to 0.2
- hamilton: float32 [576, 128], P('ka'), may hold values from -6 to 6
- equal_time: float32 [576, 128], P('ka'), may hold values from -0.5 to 2.5, as said below
- quad_class: int32 [1024], P('hist'), may hold values from 0 to 3
- live_count: int32 [16], P('hist'), may hold values from 1 to 64
Outputs:
- green_next: float32 [1024, 576, 128], P('hist', 'ka')
Inputs may be any that keep to these rules, and one draw needn't show every extreme that they name: `quad_class`: class c selects the weight q[c] of q = (0.375, 1.1666666, 0.9583333, 1.0). Stored times at positions live_count[j] or later inside block j carry no weight. `equal_time`: the imaginary diagonal entries are positive.
All inputs are finite; a program needn't handle non-finite values.
Results may differ from a plain program's by a relative error of at most 0.00005.
Values sent between devices are 32-bit elements; how exact they have to be, the bound alone decides.
A program may use at most 64 MiB of HBM per device.

v0:
```python
import functools
import math

import jax
import jax.numpy as jnp
import numpy as np
from jax import lax
from jax.experimental import pallas as pl
from jax.experimental.pallas import tpu as pltpu
from jax.sharding import PartitionSpec as P

SIDE = 24
NK = SIDE * SIDE
TIME_STEP = 0.1
HUBBARD = 1.0
QUADRATURE = (0.375, 1.1666666, 0.9583333, 1.0)
MESH = pl.DeviceIdType.MESH
KA, HIST = 32, 16
NB = NK // KA
BLK = NK // 4

OFFSETS = sorted(
    ((dx, dy, dc) for dx in range(4) for dy in range(4) for dc in range(2) if dx or dy or dc),
    key=lambda p: -(min(p[0], 4 - p[0]) + min(p[1], 4 - p[1])),
)


def phase_tables():
    k = np.arange(NK)
    out = np.zeros((4, SIDE, 2 * NK), np.float64)
    for r in range(SIDE):
        t1 = 2 * math.pi * ((r * (k // SIDE)) % SIDE) / SIDE
        t2 = 2 * math.pi * ((r * (k % SIDE)) % SIDE) / SIDE
        c1, s1, c2, s2 = np.cos(t1), np.sin(t1), np.cos(t2), np.sin(t2)
        out[0, r] = np.concatenate([c1, s1]) / SIDE
        out[1, r] = np.concatenate([s1, -c1]) / SIDE
        out[2, r] = np.concatenate([c2, c2])
        out[3, r] = np.concatenate([s2, s2])
    return out.astype(np.float32)


def contract_table():
    out = np.zeros((16 * 128, 128), np.float32)
    for d in range(16):
        for i in range(128):
            p, a = i // 64, (i // 8) % 8
            block = (i // 8 + d) % 16
            q, c = block // 8, block % 8
            if p == q:
                out[d * 128 + i, 8 * a + c] = -1.0
            else:
                out[d * 128 + i, 64 + 8 * a + c] = 1.0 if p == 0 else -1.0
    return out


def spread_table():
    out = np.zeros((128, 16 * 128), np.float32)
    for p in range(2):
        for b in range(8):
            for q in range(2):
                for a in range(8):
                    for c in range(8):
                        col = (p * 8 + b) * 128 + q * 64 + a * 8 + c
                        if p == q:
                            out[64 + a * 8 + b, col] = 1.0
                        else:
                            out[a * 8 + b, col] = 1.0 if q == 0 else -1.0
    return out


def split(v):
    high = v.astype(jnp.bfloat16)
    return high, (v - high.astype(jnp.float32)).astype(jnp.bfloat16)


def dot(a, b):
    return jnp.dot(a, b, preferred_element_type=jnp.float32)


def dot3(ah, al, bh, bl):
    return dot(ah, bh) + (dot(al, bh) + dot(ah, bl))


def collide_kernel(
    g, w, ham, eq, qc, lc, tab, con, out,
    rg, rw, tabv, conv, mh, ml, yh, yl, lat, sig, gr, pr, part, tsum, hbuf,
    send, recv, lsem,
):
    me = lax.axis_index("ka")
    z = lax.axis_index("hist")
    x, y, c = me // 8, (me // 2) % 4, me % 2

    def peer(dx, dy, dc):
        return (lax.rem(x + dx, 4) * 4 + lax.rem(y + dy, 4)) * 2 + lax.rem(c + dc, 2)

    tab_copy = pltpu.make_async_copy(tab, tabv, lsem.at[0])
    con_copy = pltpu.make_async_copy(con, conv, lsem.at[1])
    barrier = pltpu.get_barrier_semaphore()
    for d in OFFSETS:
        pl.semaphore_signal(barrier, inc=1, device_id={"ka": peer(*d)}, device_id_type=MESH)
    for d in range(1, HIST):
        pl.semaphore_signal(barrier, inc=1, device_id={"hist": lax.rem(z + d, HIST)}, device_id_type=MESH)
    tab_copy.start()
    con_copy.start()
    pl.semaphore_wait(barrier, KA - 1 + HIST - 1)

    for n, (src, dst) in enumerate(((g, rg), (w, rw))):
        for d in OFFSETS:
            to = peer(*d)
            pltpu.make_async_remote_copy(
                src_ref=src.at[:, to], dst_ref=dst.at[me], send_sem=send.at[n], recv_sem=recv.at[n],
                device_id={"ka": to}, device_id_type=MESH,
            ).start()
        pltpu.make_async_copy(src.at[:, me], dst.at[me], recv.at[n]).start()

    def arrived(n, dst):
        pltpu.make_async_copy(dst, dst, recv.at[n]).wait()

    lane = lax.broadcasted_iota(jnp.int32, (8, 128), 1)
    sign = jnp.where(lane < 64, jnp.float32(1.0), jnp.float32(-1.0))

    tab_copy.wait()

    def build(i, _):
        rows = []
        for h in range(2):
            r1 = 2 * i + h
            a1, b1 = tabv[0, pl.ds(r1, 1), :], tabv[1, pl.ds(r1, 1), :]
            rows.append(a1 * tabv[2] - b1 * tabv[3])
        high, low = split(jnp.concatenate(rows, axis=0))
        at = pl.ds(pl.multiple_of(48 * i, 16), 48)
        mh[at, :] = high
        ml[at, :] = low
        return 0

    lax.fori_loop(0, SIDE // 2, build, 0)

    def weight(t):
        s = 2 * me + t
        q = qc[s]
        value = jnp.float32(0.0)
        for i in range(4):
            value = jnp.where(q == i, jnp.float32(np.float32(TIME_STEP) * np.float32(QUADRATURE[i])), value)
        return jnp.where(s < lc[0], value, jnp.float32(0.0))

    weights = (weight(0), weight(1))
    sign16 = jnp.concatenate([sign, sign], axis=0)
    rg2, rw2 = rg.reshape(2 * NK, 128), rw.reshape(2 * NK, 128)

    arrived(0, rg)

    def stage(i, _):
        at = pl.ds(pl.multiple_of(16 * i, 16), 16)
        at2 = pl.ds(pl.multiple_of(16 * i, 16) + NK, 16)
        for t in range(2):
            v = rg2[pl.ds(32 * i + t, 16, stride=2), :]
            turned = pltpu.roll(v, 64, 1) * sign16
            col = pl.ds(128 * t, 128)
            yh[at, col], yl[at, col] = split(v)
            yh[at2, col], yl[at2, col] = split(turned)
        return 0

    lax.fori_loop(0, NK // 16, stage, 0)

    def forward(i, _):
        at = pl.ds(pl.multiple_of(BLK * i, 16), BLK)
        lat[at, :] = dot3(mh[at, :], ml[at, :], yh[...], yl[...])
        return 0

    lax.fori_loop(0, 4, forward, 0)

    def rolled(i, _):
        at = pl.ds(pl.multiple_of(8 * i, 8), 8)
        for t in range(2):
            v = rg2[pl.ds(16 * i + t, 8, stride=2), :] * weights[t]
            for d in range(16):
                gr[t, d, at, :] = pltpu.roll(v, 128 - 8 * d, 1) if d else v
        return 0

    lax.fori_loop(0, NK // 8, rolled, 0)
    con_copy.wait()
    diag = (lax.broadcasted_iota(jnp.int32, (NB, 128), 1) - 64) % 9 == 0
    diag = diag & (lax.broadcasted_iota(jnp.int32, (NB, 128), 1) >= 64)
    occupied = jnp.sum(jnp.where(diag, eq[...], jnp.float32(0.0)))
    lane1 = lax.broadcasted_iota(jnp.int32, (1, 128), 1)
    density = jnp.where((lane1 % 9 == 0) & (lane1 < 64), occupied * jnp.float32(HUBBARD / NK / HIST), jnp.float32(0.0))

    arrived(1, rw)

    def product(i, _):
        at = pl.ds(pl.multiple_of(16 * i, 16), 16)
        at2 = pl.ds(pl.multiple_of(16 * i, 16) + NK, 16)
        real = sign16 > 0
        for t in range(2):
            col = pl.ds(128 * t, 128)
            v = rw2[pl.ds(32 * i + t, 16, stride=2), :]
            l = lat[at, col]
            same = l * v
            cross = l * pltpu.roll(v, 64, 1)
            s = jnp.where(real, -cross, -same) + pltpu.roll(jnp.where(real, same, -cross), 64, 1)
            turned = pltpu.roll(s, 64, 1) * (-sign16)
            yh[at, col], yl[at, col] = split(s)
            yh[at2, col], yl[at2, col] = split(turned)
        return 0

    lax.fori_loop(0, NK // 16, product, 0)

    def back(n, _):
        blk = lax.rem(x + 3 - n, 4)
        base = pl.multiple_of(BLK * blk, 16)
        at = pl.ds(base, BLK)
        sig[...] = dot3(mh[at, :], ml[at, :], yh[...], yl[...])

        def multiply(i, _):
            rows = pl.ds(pl.multiple_of(16 * i, 16), 16)
            grow = pl.ds(pl.multiple_of(base + 16 * i, 16), 16)
            s0, s1 = sig[rows, 0:128], sig[rows, 128:256]
            for d in range(16):
                v = s0 * gr[0, d, grow, :] + s1 * gr[1, d, grow, :]
                pr[0, rows, pl.ds(128 * d, 128)], pr[1, rows, pl.ds(128 * d, 128)] = split(v)
            return 0

        lax.fori_loop(0, BLK // 16, multiply, 0)
        part[at, :] = (dot(pr[0], conv[...]) + dot(pr[1], conv[...])) + density
        for d in range(8):
            to = blk * 8 + lax.rem(2 * y + c + 7 - d, 8)

            @pl.when(to != me)
            def _():
                pltpu.make_async_remote_copy(
                    src_ref=part.at[pl.ds(NB * to, NB)], dst_ref=tsum.at[me], send_sem=send.at[2], recv_sem=recv.at[2],
                    device_id={"ka": to}, device_id_type=MESH,
                ).start()

            @pl.when(to == me)
            def _():
                pltpu.make_async_copy(part.at[pl.ds(NB * to, NB)], tsum.at[me], recv.at[2]).start()
        return 0

    lax.fori_loop(0, 4, back, 0)
    arrived(2, tsum)
    hbuf[z] = jnp.sum(tsum[...], axis=0)
    for d in (8, 7, 9, 6, 10, 5, 11, 4, 12, 3, 13, 2, 14, 1, 15):
        pltpu.make_async_remote_copy(
            src_ref=hbuf.at[z], dst_ref=hbuf.at[z], send_sem=send.at[3], recv_sem=recv.at[3],
            device_id={"hist": lax.rem(z + d, HIST)}, device_id_type=MESH,
        ).start()
    some = hbuf.at[pl.ds(0, HIST - 1)]
    pltpu.make_async_copy(some, some, recv.at[3]).wait()
    out[...] = ham[...] + jnp.sum(hbuf[...], axis=0)

    for n, ref in enumerate((rg, rw)):
        sent = ref.at[pl.ds(0, KA - 1)]
        pltpu.make_async_copy(sent, sent, send.at[n]).wait()
    sent = tsum.at[pl.ds(0, KA - 1)]
    pltpu.make_async_copy(sent, sent, send.at[2]).wait()
    pltpu.make_async_copy(some, some, send.at[3]).wait()


def propagate_kernel(eff, g, spread, out, coef):
    step = pl.program_id(0)
    per = g.shape[0]

    @pl.when(step == 0)
    def _():
        e = eff[...]
        high, rest = split(e)
        mid = (e - high.astype(jnp.float32)) - rest.astype(jnp.float32)
        low = mid.astype(jnp.bfloat16)
        full = dot(high, spread[...]) + (dot(rest, spread[...]) + dot(low, spread[...]))
        full = full * jnp.float32(TIME_STEP)
        for pb in range(16):
            coef[pb] = full[:, 128 * pb : 128 * (pb + 1)]

    lane = lax.broadcasted_iota(jnp.int32, (8, 128), 1)
    keep = lane % 8 == lax.broadcasted_iota(jnp.int32, (8, 128), 0)
    for j in range(per):
        k = step * per + j
        rows = [
            jnp.where(keep, jnp.broadcast_to(coef[pb, pl.ds(k, 1), :], (8, 128)), jnp.float32(0.0)) for pb in range(16)
        ]
        mh, ml = split(jnp.concatenate(rows, axis=0))
        v = g[j]
        vh, vl = split(v)
        out[j] = v + dot3(vh, vl, mh, ml)


def per_device(green_row, screened, hamilton, equal_time, quad_class, live_count):
    nb, tb = NB, green_row.shape[0]
    g3 = green_row.transpose(1, 0, 2)
    w3 = screened.transpose(1, 0, 2)
    f32, bf16 = jnp.float32, jnp.bfloat16
    vmem, anywhere, smem = (pl.BlockSpec(memory_space=s) for s in (pltpu.VMEM, pl.ANY, pltpu.SMEM))
    eff = pl.pallas_call(
        collide_kernel,
        out_shape=jax.ShapeDtypeStruct((nb, 128), f32),
        in_specs=[anywhere, anywhere, vmem, vmem, smem, smem, anywhere, anywhere],
        out_specs=vmem,
        scratch_shapes=[
            pltpu.VMEM((KA, nb, 2, 128), f32),
            pltpu.VMEM((KA, nb, 2, 128), f32),
            pltpu.VMEM((4, SIDE, 2 * NK), f32),
            pltpu.VMEM((2048, 128), bf16),
            pltpu.VMEM((NK, 2 * NK), bf16),
            pltpu.VMEM((NK, 2 * NK), bf16),
            pltpu.VMEM((2 * NK, 256), bf16),
            pltpu.VMEM((2 * NK, 256), bf16),
            pltpu.VMEM((NK, 256), f32),
            pltpu.VMEM((BLK, 256), f32),
            pltpu.VMEM((2, 16, NK, 128), f32),
            pltpu.VMEM((2, BLK, 2048), bf16),
            pltpu.VMEM((NK, 128), f32),
            pltpu.VMEM((KA, nb, 128), f32),
            pltpu.VMEM((HIST, nb, 128), f32),
            pltpu.SemaphoreType.DMA((4,)),
            pltpu.SemaphoreType.DMA((4,)),
            pltpu.SemaphoreType.DMA((2,)),
        ],
        compiler_params=pltpu.CompilerParams(collective_id=0, has_side_effects=True, vmem_limit_bytes=48 << 20),
        name="collide",
    )(
        g3.reshape(nb, KA, 2, 128), w3.reshape(nb, KA, 2, 128), hamilton, equal_time, quad_class, live_count,
        jnp.asarray(phase_tables()), jnp.asarray(contract_table(), dtype=bf16),
    )
    per = 3
    stepped = pl.pallas_call(
        propagate_kernel,
        out_shape=jax.ShapeDtypeStruct((nb, tb, 128), f32),
        grid=(nb // per,),
        in_specs=[
            pl.BlockSpec((nb, 128), lambda i: (0, 0)),
            pl.BlockSpec((per, tb, 128), lambda i: (i, 0, 0)),
            pl.BlockSpec((128, 2048), lambda i: (0, 0)),
        ],
        out_specs=pl.BlockSpec((per, tb, 128), lambda i: (i, 0, 0)),
        scratch_shapes=[pltpu.VMEM((16, nb, 128), f32)],
        name="propagate",
    )(eff, g3, jnp.asarray(spread_table(), dtype=bf16))
    return stepped.transpose(1, 0, 2)


def solution(mesh):
    in_specs = (
        P("hist", "ka", None), P("hist", "ka", None), P("ka", None), P("ka", None), P("hist"), P("hist"),
    )
    return jax.shard_map(
        per_device, mesh=mesh, in_specs=in_specs, out_specs=P("hist", "ka", None), check_vma=False
    )
```

profile of v0, /device:TPU:1, one launch (start us, length us, event | category | flops | bytes accessed | tf_op | source)
XLA Modules:
  0.0 83.3 jit_solution(11282483850383868540)
XLA Ops:
  0.7 0.0 copy-start.7
  0.7 0.6 copy-done.7
  1.3 0.0 copy-start
  1.3 1.1 %copy-done = f32[64,18,128]{2,0,1:T(8,128)S(1)} copy-done((f32[64,18,128]{2,0,1:T(8,128)S(1)}, f32[64,18,128]{2,0,1:T(8,128)}, u32[]{:S(2)}) %copy-start) | copy-done | bytes 589848
  2.4 0.0 copy-start.1
  2.4 1.1 %copy-done.1 = f32[64,18,128]{2,0,1:T(8,128)S(1)} copy-done((f32[64,18,128]{2,0,1:T(8,128)S(1)}, f32[64,18,128]{2,0,1:T(8,128)}, u32[]{:S(2)}) %copy-start.1) | copy-done | bytes 589848
  3.4 0.0 copy-start.2
  3.4 1.0 %copy-done.2 = bf16[2048,128]{1,0:T(8,128)(2,1)S(1)} copy-done((bf16[2048,128]{1,0:T(8,128)(2,1)S(1)}, bf16[2048,128]{1,0:T(8,128)(2,1)}, u32[]{:S(2)}) %copy-start.2) | copy-done | bytes 524312
  4.5 0.0 copy-start.3
  4.5 1.0 %copy-done.3 = f32[4,24,1152]{2,1,0:T(8,128)S(1)} copy-done((f32[4,24,1152]{2,1,0:T(8,128)S(1)}, f32[4,24,1152]{2,1,0:T(8,128)}, u32[]{:S(2)}) %copy-start.3) | copy-done | bytes 442392
  5.5 0.0 copy-start.5
  5.5 0.7 copy-done.5
  6.2 0.0 copy-start.6
  6.2 0.7 copy-done.6
  6.9 70.5 %collide.1.eff = f32[18,128]{1,0:T(8,128)S(1)} custom-call(f32[18,32,2,128]{3,2,1,0:T(2,128)S(1)} %bitcast.8, f32[18,32,2,128]{3,2,1,0:T(2,128)S(1)} %bitcast.9, f32[18,128]{1,0:T(8,128)S(1)} %copy-done.5, f32[18,128]{1,0:T(8,128)S(1)} %copy-done.6, s32[64]{0:T(128)S(1)} %copy-done.7, s32[1]{0:T(128)S(6)} %copy.10.lc, f32[4,24,1152]{2,1,0:T(8,128)S(1)} %copy-done.3, ...), custom_call_target="tpu_custom_call" | custom-call | tf_op jit(solution)/shard_map/collide/pallas_call | solution.py:294
  77.4 0.0 copy-start.4
  77.4 0.6 copy-done.4
  78.0 5.3 %propagate.1 = f32[18,64,128]{2,1,0:T(8,128)} custom-call(f32[18,128]{1,0:T(8,128)} %copy-done.4, f32[18,64,128]{2,1,0:T(8,128)} %bitcast.7, bf16[128,2048]{1,0:T(8,128)(2,1)} %constant.8.clone.spread), custom_call_target="tpu_custom_call" | custom-call | tf_op jit(solution)/shard_map/propagate/pallas_call | solution.py:326
Async XLA Ops:
  0.7 0.7 copy-start.7
  1.3 1.1 %copy-start = (f32[64,18,128]{2,0,1:T(8,128)S(1)}, f32[64,18,128]{2,0,1:T(8,128)}, u32[]{:S(2)}) copy-start(f32[64,18,128]{2,0,1:T(8,128)} %param.9) | copy-start | bytes 1769476
  2.4 1.1 %copy-start.1 = (f32[64,18,128]{2,0,1:T(8,128)S(1)}, f32[64,18,128]{2,0,1:T(8,128)}, u32[]{:S(2)}) copy-start(f32[64,18,128]{2,0,1:T(8,128)} %param.10) | copy-start | bytes 1769476
  3.4 1.0 %copy-start.2 = (bf16[2048,128]{1,0:T(8,128)(2,1)S(1)}, bf16[2048,128]{1,0:T(8,128)(2,1)}, u32[]{:S(2)}) copy-start(bf16[2048,128]{1,0:T(8,128)(2,1)} %constant.7.clone.con) | copy-start | bytes 1572868
  4.5 1.0 %copy-start.3 = (f32[4,24,1152]{2,1,0:T(8,128)S(1)}, f32[4,24,1152]{2,1,0:T(8,128)}, u32[]{:S(2)}) copy-start(f32[4,24,1152]{2,1,0:T(8,128)} %constant.6.clone.tab) | copy-start | bytes 1327108
  5.5 0.7 copy-start.5
  6.2 0.7 copy-start.6
  77.4 0.6 copy-start.4
where the time goes:
time: 83.8 us; the launch traced here: 83.3 us
  Pallas kernels  75.8 us (90%)
  local copies, waits for them, and re-layouts  6.83 us (8%)
    pallas_call x1, Pallas kernels, per_device(): pl.pallas_call(collide_kernel, out_shape=jax.ShapeDtypeStruct((nb, 128),...  70.5 us
    unnamed x16, local copies, waits for them, and re-layouts  6.83 us
    pallas_call x1, Pallas kernels, per_device(): pl.pallas_call(propagate_kernel, out_shape=jax.ShapeDtypeStruct((nb, tb,...  5.27 us

commit v1 on v0

v1 whole, which is shorter than its diff:
```python
import functools
import math

import jax
import jax.numpy as jnp
import numpy as np
from jax import lax
from jax.experimental import pallas as pl
from jax.experimental.pallas import tpu as pltpu
from jax.sharding import PartitionSpec as P

SIDE = 24
NK = SIDE * SIDE
TIME_STEP = 0.1
HUBBARD = 1.0
QUADRATURE = (0.375, 1.1666666, 0.9583333, 1.0)
MESH = pl.DeviceIdType.MESH
KA, HIST = 32, 16
NB = NK // KA
BLK = NK // 4

OFFSETS = sorted(
    ((dx, dy, dc) for dx in range(4) for dy in range(4) for dc in range(2) if dx or dy or dc),
    key=lambda p: -(min(p[0], 4 - p[0]) + min(p[1], 4 - p[1])),
)


def phase_tables():
    k = np.arange(NK)
    out = np.zeros((4, SIDE, 2 * NK), np.float64)
    for r in range(SIDE):
        t1 = 2 * math.pi * ((r * (k // SIDE)) % SIDE) / SIDE
        t2 = 2 * math.pi * ((r * (k % SIDE)) % SIDE) / SIDE
        c1, s1, c2, s2 = np.cos(t1), np.sin(t1), np.cos(t2), np.sin(t2)
        out[0, r] = np.concatenate([c1, s1]) / SIDE
        out[1, r] = np.concatenate([s1, -c1]) / SIDE
        out[2, r] = np.concatenate([c2, c2])
        out[3, r] = np.concatenate([s2, s2])
    return out.astype(np.float32)


def contract_table():
    out = np.zeros((16 * 128, 128), np.float32)
    for d in range(16):
        for i in range(128):
            p, a = i // 64, (i // 8) % 8
            block = (i // 8 + d) % 16
            q, c = block // 8, block % 8
            if p == q:
                out[d * 128 + i, 8 * a + c] = -1.0
            else:
                out[d * 128 + i, 64 + 8 * a + c] = 1.0 if p == 0 else -1.0
    return out


def split(v):
    high = v.astype(jnp.bfloat16)
    return high, (v - high.astype(jnp.float32)).astype(jnp.bfloat16)


def dot(a, b):
    return jnp.dot(a, b, preferred_element_type=jnp.float32)


def dot3(ah, al, bh, bl):
    return dot(ah, bh) + (dot(al, bh) + dot(ah, bl))


def collide_kernel(
    g, w, ham_in, eq_in, qc_in, lc, tab, con, out,
    ham, eq, qc, rg, rw, tabv, conv, mh, ml, yh, yl, lat, sig, gr, pr, part, tsum, hbuf,
    send, recv, lsem, go,
):
    me = lax.axis_index("ka")
    z = lax.axis_index("hist")
    x, y, c = me // 8, (me // 2) % 4, me % 2

    def peer(dx, dy, dc):
        return (lax.rem(x + dx, 4) * 4 + lax.rem(y + dy, 4)) * 2 + lax.rem(c + dc, 2)

    tab_copy = pltpu.make_async_copy(tab, tabv, lsem.at[0])
    con_copy = pltpu.make_async_copy(con, conv, lsem.at[1])
    small = [
        pltpu.make_async_copy(a, b, lsem.at[2 + i]) for i, (a, b) in enumerate(((qc_in, qc), (ham_in, ham), (eq_in, eq)))
    ]
    barrier = pltpu.get_barrier_semaphore()
    chip = me // 2
    for d in range(1, 16):
        pl.semaphore_signal(barrier, inc=1, device_id={"ka": 2 * lax.rem(chip + d, 16)}, device_id_type=MESH)

    @pl.when(c == 1)
    def _():
        pl.semaphore_signal(barrier, inc=1, device_id={"ka": me - 1}, device_id_type=MESH)

    tab_copy.start()
    con_copy.start()
    for copy in small:
        copy.start()

    @pl.when(c == 0)
    def _():
        pl.semaphore_wait(barrier, KA - 1)
        pl.semaphore_signal(go.at[0], inc=1, device_id={"ka": me + 1}, device_id_type=MESH)

    @pl.when(c == 1)
    def _():
        pl.semaphore_wait(go.at[0], 1)

    for n, (src, dst) in enumerate(((g, rg), (w, rw))):
        for d in OFFSETS:
            to = peer(*d)
            pltpu.make_async_remote_copy(
                src_ref=src.at[:, to], dst_ref=dst.at[me], send_sem=send.at[n], recv_sem=recv.at[n],
                device_id={"ka": to}, device_id_type=MESH,
            ).start()
        pltpu.make_async_copy(src.at[:, me], dst.at[me], recv.at[n]).start()

    @pl.when(c == 1)
    def _():
        for d in range(1, HIST):
            pl.semaphore_signal(barrier, inc=1, device_id={"hist": lax.rem(z + d, HIST)}, device_id_type=MESH)

    def arrived(n, dst):
        pltpu.make_async_copy(dst, dst, recv.at[n]).wait()

    lane = lax.broadcasted_iota(jnp.int32, (8, 128), 1)
    sign = jnp.where(lane < 64, jnp.float32(1.0), jnp.float32(-1.0))

    tab_copy.wait()

    def build(i, _):
        rows = []
        for h in range(2):
            r1 = 2 * i + h
            a1, b1 = tabv[0, pl.ds(r1, 1), :], tabv[1, pl.ds(r1, 1), :]
            rows.append(a1 * tabv[2] - b1 * tabv[3])
        high, low = split(jnp.concatenate(rows, axis=0))
        at = pl.ds(pl.multiple_of(48 * i, 16), 48)
        mh[at, :] = high
        ml[at, :] = low
        return 0

    lax.fori_loop(0, SIDE // 2, build, 0)

    for copy in small:
        copy.wait()

    def weight(t):
        s = 2 * me + t
        q = qc[s]
        value = jnp.float32(0.0)
        for i in range(4):
            value = jnp.where(q == i, jnp.float32(np.float32(TIME_STEP) * np.float32(QUADRATURE[i])), value)
        return jnp.where(s < lc[0], value, jnp.float32(0.0))

    weights = (weight(0), weight(1))
    sign16 = jnp.concatenate([sign, sign], axis=0)
    rg2, rw2 = rg.reshape(2 * NK, 128), rw.reshape(2 * NK, 128)

    arrived(0, rg)

    def stage(i, _):
        for u in range(3):
            row = pl.multiple_of(48 * i + 16 * u, 16)
            at, at2 = pl.ds(row, 16), pl.ds(row + NK, 16)
            for t in range(2):
                v = rg2[pl.ds(2 * row + t, 16, stride=2), :]
                turned = pltpu.roll(v, 64, 1) * sign16
                col = pl.ds(128 * t, 128)
                yh[at, col], yl[at, col] = split(v)
                yh[at2, col], yl[at2, col] = split(turned)
        return 0

    lax.fori_loop(0, NK // 48, stage, 0)

    def forward(i, _):
        at = pl.ds(pl.multiple_of(BLK * i, 16), BLK)
        v = dot3(mh[at, :], ml[at, :], yh[...], yl[...])
        lat[0, at, :] = v
        for t in range(2):
            lat[1, at, pl.ds(128 * t, 128)] = pltpu.roll(v[:, 128 * t : 128 * (t + 1)], 64, 1)
        return 0

    lax.fori_loop(0, 4, forward, 0)

    def rolled(i, _):
        for u in range(4):
            row = pl.multiple_of(32 * i + 8 * u, 8)
            for t in range(2):
                v = rg2[pl.ds(2 * row + t, 8, stride=2), :] * weights[t]
                for d in range(16):
                    gr[t, d, pl.ds(row, 8), :] = pltpu.roll(v, 128 - 8 * d, 1) if d else v
        return 0

    lax.fori_loop(0, NK // 32, rolled, 0)
    con_copy.wait()
    diag = (lax.broadcasted_iota(jnp.int32, (NB, 128), 1) - 64) % 9 == 0
    diag = diag & (lax.broadcasted_iota(jnp.int32, (NB, 128), 1) >= 64)
    occupied = jnp.sum(jnp.where(diag, eq[...], jnp.float32(0.0)))
    lane1 = lax.broadcasted_iota(jnp.int32, (1, 128), 1)
    density = jnp.where((lane1 % 9 == 0) & (lane1 < 64), occupied * jnp.float32(HUBBARD / NK / HIST), jnp.float32(0.0))

    arrived(1, rw)

    real = sign16 > 0

    def product(i, _):
        for u in range(3):
            row = pl.multiple_of(48 * i + 16 * u, 16)
            at, at2 = pl.ds(row, 16), pl.ds(row + NK, 16)
            for t in range(2):
                col = pl.ds(128 * t, 128)
                v = rw2[pl.ds(2 * row + t, 16, stride=2), :]
                same, cross = lat[0, at, col] * v, lat[1, at, col] * v
                own = -jnp.where(real, cross, same)
                other = jnp.where(real, same, -cross)
                s = own + pltpu.roll(other, 64, 1)
                turned = -sign16 * (pltpu.roll(own, 64, 1) + other)
                yh[at, col], yl[at, col] = split(s)
                yh[at2, col], yl[at2, col] = split(turned)
        return 0

    lax.fori_loop(0, NK // 48, product, 0)

    def back(n, _):
        blk = lax.rem(x + 3 - n, 4)
        base = pl.multiple_of(BLK * blk, 16)
        at = pl.ds(base, BLK)
        sig[...] = dot3(mh[at, :], ml[at, :], yh[...], yl[...])

        def multiply(i, _):
            for u in range(3):
                rows = pl.ds(pl.multiple_of(48 * i + 16 * u, 16), 16)
                grow = pl.ds(pl.multiple_of(base + 48 * i + 16 * u, 16), 16)
                s0, s1 = sig[rows, 0:128], sig[rows, 128:256]
                for d in range(16):
                    v = s0 * gr[0, d, grow, :] + s1 * gr[1, d, grow, :]
                    pr[0, rows, pl.ds(128 * d, 128)], pr[1, rows, pl.ds(128 * d, 128)] = split(v)
            return 0

        lax.fori_loop(0, BLK // 48, multiply, 0)
        part[at, :] = (dot(pr[0], conv[...]) + dot(pr[1], conv[...])) + density
        for d in range(8):
            to = blk * 8 + lax.rem(2 * y + c + 7 - d, 8)

            @pl.when(to != me)
            def _():
                pltpu.make_async_remote_copy(
                    src_ref=part.at[pl.ds(NB * to, NB)], dst_ref=tsum.at[me], send_sem=send.at[2], recv_sem=recv.at[2],
                    device_id={"ka": to}, device_id_type=MESH,
                ).start()

            @pl.when(to == me)
            def _():
                pltpu.make_async_copy(part.at[pl.ds(NB * to, NB)], tsum.at[me], recv.at[2]).start()
        return 0

    lax.fori_loop(0, 4, back, 0)

    @pl.when(c == 1)
    def _():
        pl.semaphore_wait(barrier, HIST - 1)
        pl.semaphore_signal(go.at[1], inc=1, device_id={"ka": me - 1}, device_id_type=MESH)

    arrived(2, tsum)
    hbuf[z] = jnp.sum(tsum[...], axis=0)

    @pl.when(c == 0)
    def _():
        pl.semaphore_wait(go.at[1], 1)

    for d in (8, 7, 9, 6, 10, 5, 11, 4, 12, 3, 13, 2, 14, 1, 15):
        pltpu.make_async_remote_copy(
            src_ref=hbuf.at[z], dst_ref=hbuf.at[z], send_sem=send.at[3], recv_sem=recv.at[3],
            device_id={"hist": lax.rem(z + d, HIST)}, device_id_type=MESH,
        ).start()
    some = hbuf.at[pl.ds(0, HIST - 1)]
    pltpu.make_async_copy(some, some, recv.at[3]).wait()
    out[pl.ds(0, NB), :] = ham[...] + jnp.sum(hbuf[...], axis=0)
    out[pl.ds(NB, 24 - NB), :] = jnp.zeros((24 - NB, 128), jnp.float32)

    for n, ref in enumerate((rg, rw)):
        sent = ref.at[pl.ds(0, KA - 1)]
        pltpu.make_async_copy(sent, sent, send.at[n]).wait()
    sent = tsum.at[pl.ds(0, KA - 1)]
    pltpu.make_async_copy(sent, sent, send.at[2]).wait()
    pltpu.make_async_copy(some, some, send.at[3]).wait()


def propagate_kernel(eff, g, out, gv, ov, coef, sem):
    nb = g.shape[0]
    groups = 3
    per = nb // groups
    fetch = [pltpu.make_async_copy(g.at[pl.ds(per * i, per)], gv.at[pl.ds(per * i, per)], sem.at[i]) for i in range(groups)]
    for copy in fetch:
        copy.start()

    e = eff[...] * jnp.float32(TIME_STEP)
    lane = lax.broadcasted_iota(jnp.int32, e.shape, 1)
    second = lane // 64
    for p in range(2):
        for b in range(8):
            from_imag = second == p
            index = jnp.where(from_imag, 64, 0) + (lane // 8) % 8 * 8 + b
            v = jnp.take_along_axis(e, index, axis=1)
            coef[8 * p + b] = jnp.where(from_imag | (second == 0), v, -v)

    lane8 = lax.broadcasted_iota(jnp.int32, (8, 128), 1)
    keep = lane8 % 8 == lax.broadcasted_iota(jnp.int32, (8, 128), 0)
    flush = []
    for i in range(groups):
        fetch[i].wait()
        for k in range(per * i, per * (i + 1)):
            rows = [
                jnp.where(keep, jnp.broadcast_to(coef[pb, pl.ds(k, 1), :], (8, 128)), jnp.float32(0.0)) for pb in range(16)
            ]
            mh, ml = split(jnp.concatenate(rows, axis=0))
            v = gv[k]
            vh, vl = split(v)
            ov[k] = v + dot3(vh, vl, mh, ml)
        copy = pltpu.make_async_copy(ov.at[pl.ds(per * i, per)], out.at[pl.ds(per * i, per)], sem.at[groups + i])
        copy.start()
        flush.append(copy)
    for copy in flush:
        copy.wait()


def per_device(green_row, screened, hamilton, equal_time, quad_class, live_count):
    nb, tb = NB, green_row.shape[0]
    g3 = green_row.transpose(1, 0, 2)
    w3 = screened.transpose(1, 0, 2)
    f32, bf16 = jnp.float32, jnp.bfloat16
    vmem, hbm, smem = (pl.BlockSpec(memory_space=s) for s in (pltpu.VMEM, pltpu.HBM, pltpu.SMEM))
    eff = pl.pallas_call(
        collide_kernel,
        out_shape=jax.ShapeDtypeStruct((24, 128), f32),
        in_specs=[hbm, hbm, hbm, hbm, hbm, smem, hbm, hbm],
        out_specs=vmem,
        scratch_shapes=[
            pltpu.VMEM((nb, 128), f32),
            pltpu.VMEM((nb, 128), f32),
            pltpu.SMEM((tb,), jnp.int32),
            pltpu.VMEM((KA, nb, 2, 128), f32),
            pltpu.VMEM((KA, nb, 2, 128), f32),
            pltpu.VMEM((4, SIDE, 2 * NK), f32),
            pltpu.VMEM((2048, 128), bf16),
            pltpu.VMEM((NK, 2 * NK), bf16),
            pltpu.VMEM((NK, 2 * NK), bf16),
            pltpu.VMEM((2 * NK, 256), bf16),
            pltpu.VMEM((2 * NK, 256), bf16),
            pltpu.VMEM((2, NK, 256), f32),
            pltpu.VMEM((BLK, 256), f32),
            pltpu.VMEM((2, 16, NK, 128), f32),
            pltpu.VMEM((2, BLK, 2048), bf16),
            pltpu.VMEM((NK, 128), f32),
            pltpu.VMEM((KA, nb, 128), f32),
            pltpu.VMEM((HIST, nb, 128), f32),
            pltpu.SemaphoreType.DMA((4,)),
            pltpu.SemaphoreType.DMA((4,)),
            pltpu.SemaphoreType.DMA((5,)),
            pltpu.SemaphoreType.REGULAR((2,)),
        ],
        compiler_params=pltpu.CompilerParams(collective_id=0, has_side_effects=True, vmem_limit_bytes=60 << 20),
        name="collide",
    )(
        g3.reshape(nb, KA, 2, 128), w3.reshape(nb, KA, 2, 128), hamilton, equal_time, quad_class, live_count,
        jnp.asarray(phase_tables()), jnp.asarray(contract_table(), dtype=bf16),
    )
    stepped = pl.pallas_call(
        propagate_kernel,
        out_shape=jax.ShapeDtypeStruct((nb, tb, 128), f32),
        in_specs=[vmem, hbm],
        out_specs=hbm,
        scratch_shapes=[
            pltpu.VMEM((nb, tb, 128), f32),
            pltpu.VMEM((nb, tb, 128), f32),
            pltpu.VMEM((16, 24, 128), f32),
            pltpu.SemaphoreType.DMA((6,)),
        ],
        name="propagate",
    )(eff, g3)
    return stepped.transpose(1, 0, 2)


def solution(mesh):
    in_specs = (
        P("hist", "ka", None), P("hist", "ka", None), P("ka", None), P("ka", None), P("hist"), P("hist"),
    )
    return jax.shard_map(
        per_device, mesh=mesh, in_specs=in_specs, out_specs=P("hist", "ka", None), check_vma=False
    )
```

time: 83.8 us -> 60.3 us (0.72)
  the two profiles are of different devices: /device:TPU:1 before, /device:TPU:2 now
where the time goes in v1:
time: 60.3 us; the launch traced here: 60.1 us
  Pallas kernels  59.4 us (99%)
  between operations  0.66 us (1%)
    pallas_call x1, Pallas kernels, per_device(): pl.pallas_call(collide_kernel, out_shape=jax.ShapeDtypeStruct((24, 128),...  56.2 us
    pallas_call x1, Pallas kernels, per_device(): pl.pallas_call(propagate_kernel, out_shape=jax.ShapeDtypeStruct((nb, tb,...  3.25 us

profile of v1, /device:TPU:2, one launch (start us, length us, event | category | flops | bytes accessed | tf_op | source)
XLA Modules:
  0.0 60.1 jit_solution(15521205364259816943)
XLA Ops:
  0.7 56.2 %collide.1.eff = f32[24,128]{1,0:T(8,128)} custom-call(f32[18,32,2,128]{3,2,1,0:T(2,128)} %bitcast.7, f32[18,32,2,128]{3,2,1,0:T(2,128)} %bitcast.9, f32[18,128]{1,0:T(8,128)} %ham_in.1, f32[18,128]{1,0:T(8,128)} %eq_in.1, s32[64]{0:T(128)} %qc_in.1, s32[1]{0:T(128)S(6)} %copy.9.lc, f32[4,24,1152]{2,1,0:T(8,128)} %constant.4.clone.tab, ...), custom_call_target="tpu_custom_call" | custom-call | tf_op jit(solution)/shard_map/collide/pallas_call | solution.py:334
  56.8 3.2 %propagate.1 = f32[18,64,128]{2,1,0:T(8,128)} custom-call(f32[24,128]{1,0:T(8,128)} %collide.1.eff, f32[18,64,128]{2,1,0:T(8,128)} %bitcast.8), custom_call_target="tpu_custom_call" | custom-call | tf_op jit(solution)/shard_map/propagate/pallas_call | solution.py:369

commit v2 on v1

--- a/solution.py
+++ b/solution.py
@@ -26,16 +26,19 @@
 
 
 def phase_tables():
-    k = np.arange(NK)
-    out = np.zeros((4, SIDE, 2 * NK), np.float64)
-    for r in range(SIDE):
-        t1 = 2 * math.pi * ((r * (k // SIDE)) % SIDE) / SIDE
-        t2 = 2 * math.pi * ((r * (k % SIDE)) % SIDE) / SIDE
-        c1, s1, c2, s2 = np.cos(t1), np.sin(t1), np.cos(t2), np.sin(t2)
-        out[0, r] = np.concatenate([c1, s1]) / SIDE
-        out[1, r] = np.concatenate([s1, -c1]) / SIDE
-        out[2, r] = np.concatenate([c2, c2])
-        out[3, r] = np.concatenate([s2, s2])
+    col = np.arange(BLK)
+    major, minor = col // SIDE, col % SIDE
+    out = np.zeros((2, 4, SIDE, 2 * BLK), np.float64)
+    for i in range(SIDE):
+        m, part = i // 6, i % 6
+        for way, turn in ((0, (4 * part + m) * major), (1, part * (4 * major + m))):
+            t1 = 2 * math.pi * (turn % SIDE) / SIDE
+            t2 = 2 * math.pi * ((i * minor) % SIDE) / SIDE
+            c1, s1, c2, s2 = np.cos(t1), np.sin(t1), np.cos(t2), np.sin(t2)
+            out[way, 0, i] = np.concatenate([c1, s1]) / SIDE
+            out[way, 1, i] = np.concatenate([s1, -c1]) / SIDE
+            out[way, 2, i] = np.concatenate([c2, c2])
+            out[way, 3, i] = np.concatenate([s2, s2])
     return out.astype(np.float32)
 
 
@@ -129,15 +132,15 @@
     tab_copy.wait()
 
     def build(i, _):
-        rows = []
-        for h in range(2):
-            r1 = 2 * i + h
-            a1, b1 = tabv[0, pl.ds(r1, 1), :], tabv[1, pl.ds(r1, 1), :]
-            rows.append(a1 * tabv[2] - b1 * tabv[3])
-        high, low = split(jnp.concatenate(rows, axis=0))
-        at = pl.ds(pl.multiple_of(48 * i, 16), 48)
-        mh[at, :] = high
-        ml[at, :] = low
+        for way in range(2):
+            rows = []
+            for h in range(2):
+                part = pl.ds(2 * i + h, 1)
+                rows.append(tabv[way, 0, part, :] * tabv[way, 2] - tabv[way, 1, part, :] * tabv[way, 3])
+            high, low = split(jnp.concatenate(rows, axis=0))
+            at = pl.ds(pl.multiple_of(48 * i, 16), 48)
+            mh[way, at, :] = high
+            ml[way, at, :] = low
         return 0
 
     lax.fori_loop(0, SIDE // 2, build, 0)
@@ -159,37 +162,44 @@
 
     arrived(0, rg)
 
+    def put(m, row, t, v, turned):
+        col = pl.ds(128 * t, 128)
+        yh[m, pl.ds(row, 16), col], yl[m, pl.ds(row, 16), col] = split(v)
+        yh[m, pl.ds(row + BLK, 16), col], yl[m, pl.ds(row + BLK, 16), col] = split(turned)
+
     def stage(i, _):
-        for u in range(3):
-            row = pl.multiple_of(48 * i + 16 * u, 16)
-            at, at2 = pl.ds(row, 16), pl.ds(row + NK, 16)
-            for t in range(2):
-                v = rg2[pl.ds(2 * row + t, 16, stride=2), :]
-                turned = pltpu.roll(v, 64, 1) * sign16
-                col = pl.ds(128 * t, 128)
-                yh[at, col], yl[at, col] = split(v)
-                yh[at2, col], yl[at2, col] = split(turned)
+        row = pl.multiple_of(16 * i, 16)
+        for t in range(2):
+            v = [rg2[pl.ds(2 * (row + BLK * j) + t, 16, stride=2), :] for j in range(4)]
+            w_ = [pltpu.roll(e, 64, 1) * sign16 for e in v]
+            even, odd, even_, odd_ = v[0] + v[2], v[1] + v[3], w_[0] + w_[2], w_[1] + w_[3]
+            put(0, row, t, even + odd, even_ + odd_)
+            put(2, row, t, even - odd, even_ - odd_)
+            even, odd, even_, odd_ = v[0] - v[2], v[1] - v[3], w_[0] - w_[2], w_[1] - w_[3]
+            put(1, row, t, even + odd_, even_ - odd)
+            put(3, row, t, even - odd_, even_ + odd)
         return 0
 
-    lax.fori_loop(0, NK // 48, stage, 0)
-
-    def forward(i, _):
-        at = pl.ds(pl.multiple_of(BLK * i, 16), BLK)
-        v = dot3(mh[at, :], ml[at, :], yh[...], yl[...])
+    lax.fori_loop(0, BLK // 16, stage, 0)
+
+    def transform(way, m):
+        at = pl.ds(BLK * m, BLK)
+        return dot3(mh[way, at, :], ml[way, at, :], yh[m], yl[m])
+
+    for m in range(4):
+        v = transform(0, m)
+        at = pl.ds(BLK * m, BLK)
         lat[0, at, :] = v
         for t in range(2):
             lat[1, at, pl.ds(128 * t, 128)] = pltpu.roll(v[:, 128 * t : 128 * (t + 1)], 64, 1)
-        return 0
-
-    lax.fori_loop(0, 4, forward, 0)
 
     def rolled(i, _):
-        for u in range(4):
-            row = pl.multiple_of(32 * i + 8 * u, 8)
+        for u in range(2):
+            row = pl.multiple_of(32 * i + 16 * u, 16)
             for t in range(2):
-                v = rg2[pl.ds(2 * row + t, 8, stride=2), :] * weights[t]
+                v = rg2[pl.ds(2 * row + t, 16, stride=2), :] * weights[t]
                 for d in range(16):
-                    gr[t, d, pl.ds(row, 8), :] = pltpu.roll(v, 128 - 8 * d, 1) if d else v
+                    gr[2 * i + u, 2 * d + t] = pltpu.roll(v, 128 - 8 * d, 1) if d else v
         return 0
 
     lax.fori_loop(0, NK // 32, rolled, 0)
@@ -205,57 +215,56 @@
     real = sign16 > 0
 
     def product(i, _):
+        m, pair = i // 3, i % 3
         for u in range(3):
-            row = pl.multiple_of(48 * i + 16 * u, 16)
-            at, at2 = pl.ds(row, 16), pl.ds(row + NK, 16)
+            row = pl.multiple_of(48 * pair + 16 * u, 16)
+            at = pl.ds(pl.multiple_of(BLK * m + 48 * pair + 16 * u, 16), 16)
             for t in range(2):
                 col = pl.ds(128 * t, 128)
-                v = rw2[pl.ds(2 * row + t, 16, stride=2), :]
+                halves = []
+                for h in range(2):
+                    e = 2 * u + h
+                    start = ((8 * pair + 4 * (e // 3) + m) * SIDE + 8 * (e % 3)) * 2 + t
+                    halves.append(rw2[pl.ds(start, 8, stride=2), :])
+                v = jnp.concatenate(halves, axis=0)
                 same, cross = lat[0, at, col] * v, lat[1, at, col] * v
                 own = -jnp.where(real, cross, same)
                 other = jnp.where(real, same, -cross)
-                s = own + pltpu.roll(other, 64, 1)
-                turned = -sign16 * (pltpu.roll(own, 64, 1) + other)
-                yh[at, col], yl[at, col] = split(s)
-                yh[at2, col], yl[at2, col] = split(turned)
+                put(m, row, t, own + pltpu.roll(other, 64, 1), -sign16 * (pltpu.roll(own, 64, 1) + other))
         return 0
 
-    lax.fori_loop(0, NK // 48, product, 0)
-
-    def back(n, _):
-        blk = lax.rem(x + 3 - n, 4)
-        base = pl.multiple_of(BLK * blk, 16)
-        at = pl.ds(base, BLK)
-        sig[...] = dot3(mh[at, :], ml[at, :], yh[...], yl[...])
-
-        def multiply(i, _):
-            for u in range(3):
-                rows = pl.ds(pl.multiple_of(48 * i + 16 * u, 16), 16)
-                grow = pl.ds(pl.multiple_of(base + 48 * i + 16 * u, 16), 16)
-                s0, s1 = sig[rows, 0:128], sig[rows, 128:256]
-                for d in range(16):
-                    v = s0 * gr[0, d, grow, :] + s1 * gr[1, d, grow, :]
-                    pr[0, rows, pl.ds(128 * d, 128)], pr[1, rows, pl.ds(128 * d, 128)] = split(v)
-            return 0
-
-        lax.fori_loop(0, BLK // 48, multiply, 0)
-        part[at, :] = (dot(pr[0], conv[...]) + dot(pr[1], conv[...])) + density
-        for d in range(8):
-            to = blk * 8 + lax.rem(2 * y + c + 7 - d, 8)
-
-            @pl.when(to != me)
-            def _():
-                pltpu.make_async_remote_copy(
-                    src_ref=part.at[pl.ds(NB * to, NB)], dst_ref=tsum.at[me], send_sem=send.at[2], recv_sem=recv.at[2],
-                    device_id={"ka": to}, device_id_type=MESH,
-                ).start()
-
-            @pl.when(to == me)
-            def _():
-                pltpu.make_async_copy(part.at[pl.ds(NB * to, NB)], tsum.at[me], recv.at[2]).start()
-        return 0
-
-    lax.fori_loop(0, 4, back, 0)
+    lax.fori_loop(0, 12, product, 0)
+
+    e = [transform(1, m) for m in range(4)]
+    diff = e[1] - e[3]
+    across = [pltpu.roll(diff[:, 128 * t : 128 * (t + 1)], 64, 1) for t in range(2)]
+    turn = jnp.where(lax.broadcasted_iota(jnp.int32, (BLK, 128), 1) < 64, jnp.float32(-1.0), jnp.float32(1.0))
+    diff = jnp.concatenate([turn * part_ for part_ in across], axis=1)
+    sig[0] = (e[0] + e[2]) + (e[1] + e[3])
+    sig[2] = (e[0] + e[2]) - (e[1] + e[3])
+    sig[1] = (e[0] - e[2]) + diff
+    sig[3] = (e[0] - e[2]) - diff
+
+    def block(n):
+        return lax.rem(x + 3 - n, 4)
+
+    for n in range(4):
+        for i in range(BLK // 16):
+            rows = pl.ds(16 * i, 16)
+            s0, s1 = sig[block(n), rows, 0:128], sig[block(n), rows, 128:256]
+            group = (BLK // 16) * block(n) + i
+            for d in range(16):
+                v = s0 * gr[group, 2 * d] + s1 * gr[group, 2 * d + 1]
+                pr[n % 2, 0, rows, pl.ds(128 * d, 128)], pr[n % 2, 1, rows, pl.ds(128 * d, 128)] = split(v)
+        at = pl.ds(pl.multiple_of(BLK * block(n), 16), BLK)
+        part[at, :] = (dot(pr[n % 2, 0], conv[...]) + dot(pr[n % 2, 1], conv[...])) + density
+        for d in range(8 if n < 3 else 7):
+            to = block(n) * 8 + lax.rem(2 * y + c + 4 + d if n < 3 else 2 * y + c + 1 + d, 8)
+            pltpu.make_async_remote_copy(
+                src_ref=part.at[pl.ds(NB * to, NB)], dst_ref=tsum.at[me], send_sem=send.at[2], recv_sem=recv.at[2],
+                device_id={"ka": to}, device_id_type=MESH,
+            ).start()
+    pltpu.make_async_copy(part.at[pl.ds(NB * me, NB)], tsum.at[me], recv.at[2]).start()
 
     @pl.when(c == 1)
     def _():
@@ -342,16 +351,16 @@
             pltpu.SMEM((tb,), jnp.int32),
             pltpu.VMEM((KA, nb, 2, 128), f32),
             pltpu.VMEM((KA, nb, 2, 128), f32),
-            pltpu.VMEM((4, SIDE, 2 * NK), f32),
+            pltpu.VMEM((2, 4, SIDE, 2 * BLK), f32),
             pltpu.VMEM((2048, 128), bf16),
-            pltpu.VMEM((NK, 2 * NK), bf16),
-            pltpu.VMEM((NK, 2 * NK), bf16),
-            pltpu.VMEM((2 * NK, 256), bf16),
-            pltpu.VMEM((2 * NK, 256), bf16),
+            pltpu.VMEM((2, NK, 2 * BLK), bf16),
+            pltpu.VMEM((2, NK, 2 * BLK), bf16),
+            pltpu.VMEM((4, 2 * BLK, 256), bf16),
+            pltpu.VMEM((4, 2 * BLK, 256), bf16),
             pltpu.VMEM((2, NK, 256), f32),
-            pltpu.VMEM((BLK, 256), f32),
-            pltpu.VMEM((2, 16, NK, 128), f32),
-            pltpu.VMEM((2, BLK, 2048), bf16),
+            pltpu.VMEM((4, BLK, 256), f32),
+            pltpu.VMEM((NK // 16, 32, 16, 128), f32),
+            pltpu.VMEM((2, 2, BLK, 2048), bf16),
             pltpu.VMEM((NK, 128), f32),
             pltpu.VMEM((KA, nb, 128), f32),
             pltpu.VMEM((HIST, nb, 128), f32),

time: 60.3 us -> 55 us (0.912)
  Pallas kernels: 59.4 us -> 54.1 us
    pallas_call x1, Pallas kernels: 56.2 us -> 50.9 us  [per_device(): pl.pallas_call(collide_kernel, out_shape=jax.ShapeDtypeStruct((24, 128),...]
where the time goes in v2:
time: 55 us; the launch traced here: 54.8 us
  Pallas kernels  54.1 us (98%)
  between operations  0.66 us (1%)
    pallas_call x1, Pallas kernels, per_device(): pl.pallas_call(collide_kernel, out_shape=jax.ShapeDtypeStruct((24, 128),...  50.9 us
    pallas_call x1, Pallas kernels, per_device(): pl.pallas_call(propagate_kernel, out_shape=jax.ShapeDtypeStruct((nb, tb,...  3.25 us

profile of v2, /device:TPU:2, one launch (start us, length us, event | category | flops | bytes accessed | tf_op | source)
XLA Modules:
  0.0 54.8 jit_solution(17137091605415399139)
XLA Ops:
  0.7 50.9 %collide.1.eff = f32[24,128]{1,0:T(8,128)} custom-call(f32[18,32,2,128]{3,2,1,0:T(2,128)} %bitcast.7, f32[18,32,2,128]{3,2,1,0:T(2,128)} %bitcast.9, f32[18,128]{1,0:T(8,128)} %ham_in.1, f32[18,128]{1,0:T(8,128)} %eq_in.1, s32[64]{0:T(128)} %qc_in.1, s32[1]{0:T(128)S(6)} %copy.9.lc, f32[2,4,24,288]{3,2,1,0:T(8,128)} %constant.4.clone.tab, ...), custom_call_target="tpu_custom_call" | custom-call | tf_op jit(solution)/shard_map/collide/pallas_call | solution.py:343
  51.6 3.3 %propagate.1 = f32[18,64,128]{2,1,0:T(8,128)} custom-call(f32[24,128]{1,0:T(8,128)} %collide.1.eff, f32[18,64,128]{2,1,0:T(8,128)} %bitcast.8), custom_call_target="tpu_custom_call" | custom-call | tf_op jit(solution)/shard_map/propagate/pallas_call | solution.py:378

commit v3 on v2

--- a/solution.py
+++ b/solution.py
@@ -70,8 +70,8 @@
 
 
 def collide_kernel(
-    g, w, ham_in, eq_in, qc_in, lc, tab, con, out,
-    ham, eq, qc, rg, rw, tabv, conv, mh, ml, yh, yl, lat, sig, gr, pr, part, tsum, hbuf,
+    g, w, ham_in, eq_in, qc_in, lc_in, tab, con, out,
+    ham, eq, qc, lc, rg, rw, tabv, conv, mh, ml, yh, yl, lat, sig, gr, pr, part, tsum, hbuf,
     send, recv, lsem, go,
 ):
     me = lax.axis_index("ka")
@@ -84,7 +84,7 @@
     tab_copy = pltpu.make_async_copy(tab, tabv, lsem.at[0])
     con_copy = pltpu.make_async_copy(con, conv, lsem.at[1])
     small = [
-        pltpu.make_async_copy(a, b, lsem.at[2 + i]) for i, (a, b) in enumerate(((qc_in, qc), (ham_in, ham), (eq_in, eq)))
+        pltpu.make_async_copy(a, b, lsem.at[2 + i]) for i, (a, b) in enumerate(((qc_in, qc), (lc_in, lc), (ham_in, ham), (eq_in, eq)))
     ]
     barrier = pltpu.get_barrier_semaphore()
     chip = me // 2
@@ -154,7 +154,7 @@
         value = jnp.float32(0.0)
         for i in range(4):
             value = jnp.where(q == i, jnp.float32(np.float32(TIME_STEP) * np.float32(QUADRATURE[i])), value)
-        return jnp.where(s < lc[0], value, jnp.float32(0.0))
+        return jnp.where(s < lc[0, 0], value, jnp.float32(0.0))
 
     weights = (weight(0), weight(1))
     sign16 = jnp.concatenate([sign, sign], axis=0)
@@ -215,25 +215,26 @@
     real = sign16 > 0
 
     def product(i, _):
-        m, pair = i // 3, i % 3
-        for u in range(3):
-            row = pl.multiple_of(48 * pair + 16 * u, 16)
-            at = pl.ds(pl.multiple_of(BLK * m + 48 * pair + 16 * u, 16), 16)
-            for t in range(2):
-                col = pl.ds(128 * t, 128)
-                halves = []
-                for h in range(2):
-                    e = 2 * u + h
-                    start = ((8 * pair + 4 * (e // 3) + m) * SIDE + 8 * (e % 3)) * 2 + t
-                    halves.append(rw2[pl.ds(start, 8, stride=2), :])
-                v = jnp.concatenate(halves, axis=0)
-                same, cross = lat[0, at, col] * v, lat[1, at, col] * v
-                own = -jnp.where(real, cross, same)
-                other = jnp.where(real, same, -cross)
-                put(m, row, t, own + pltpu.roll(other, 64, 1), -sign16 * (pltpu.roll(own, 64, 1) + other))
+        for pair in range(3):
+            m = i
+            for u in range(3):
+                row = pl.multiple_of(48 * pair + 16 * u, 16)
+                at = pl.ds(pl.multiple_of(BLK * m + 48 * pair + 16 * u, 16), 16)
+                for t in range(2):
+                    col = pl.ds(128 * t, 128)
+                    halves = []
+                    for h in range(2):
+                        e = 2 * u + h
+                        start = ((8 * pair + 4 * (e // 3) + m) * SIDE + 8 * (e % 3)) * 2 + t
+                        halves.append(rw2[pl.ds(start, 8, stride=2), :])
+                    v = jnp.concatenate(halves, axis=0)
+                    same, cross = lat[0, at, col] * v, lat[1, at, col] * v
+                    own = -jnp.where(real, cross, same)
+                    other = jnp.where(real, same, -cross)
+                    put(m, row, t, own + pltpu.roll(other, 64, 1), -sign16 * (pltpu.roll(own, 64, 1) + other))
         return 0
 
-    lax.fori_loop(0, 12, product, 0)
+    lax.fori_loop(0, 4, product, 0)
 
     e = [transform(1, m) for m in range(4)]
     diff = e[1] - e[3]
@@ -296,13 +297,16 @@
     pltpu.make_async_copy(some, some, send.at[3]).wait()
 
 
-def propagate_kernel(eff, g, out, gv, ov, coef, sem):
+def propagate_kernel(eff_in, g, out, eff, gv, ov, coef, sem):
     nb = g.shape[0]
     groups = 3
     per = nb // groups
     fetch = [pltpu.make_async_copy(g.at[pl.ds(per * i, per)], gv.at[pl.ds(per * i, per)], sem.at[i]) for i in range(groups)]
+    first = pltpu.make_async_copy(eff_in, eff, sem.at[2 * groups])
+    first.start()
     for copy in fetch:
         copy.start()
+    first.wait()
 
     e = eff[...] * jnp.float32(TIME_STEP)
     lane = lax.broadcasted_iota(jnp.int32, e.shape, 1)
@@ -339,16 +343,17 @@
     g3 = green_row.transpose(1, 0, 2)
     w3 = screened.transpose(1, 0, 2)
     f32, bf16 = jnp.float32, jnp.bfloat16
-    vmem, hbm, smem = (pl.BlockSpec(memory_space=s) for s in (pltpu.VMEM, pltpu.HBM, pltpu.SMEM))
+    vmem, hbm = (pl.BlockSpec(memory_space=s) for s in (pltpu.VMEM, pltpu.HBM))
     eff = pl.pallas_call(
         collide_kernel,
         out_shape=jax.ShapeDtypeStruct((24, 128), f32),
-        in_specs=[hbm, hbm, hbm, hbm, hbm, smem, hbm, hbm],
+        in_specs=[hbm] * 8,
         out_specs=vmem,
         scratch_shapes=[
             pltpu.VMEM((nb, 128), f32),
             pltpu.VMEM((nb, 128), f32),
             pltpu.SMEM((tb,), jnp.int32),
+            pltpu.SMEM((1, 1), jnp.int32),
             pltpu.VMEM((KA, nb, 2, 128), f32),
             pltpu.VMEM((KA, nb, 2, 128), f32),
             pltpu.VMEM((2, 4, SIDE, 2 * BLK), f32),
@@ -366,25 +371,26 @@
             pltpu.VMEM((HIST, nb, 128), f32),
             pltpu.SemaphoreType.DMA((4,)),
             pltpu.SemaphoreType.DMA((4,)),
-            pltpu.SemaphoreType.DMA((5,)),
+            pltpu.SemaphoreType.DMA((6,)),
             pltpu.SemaphoreType.REGULAR((2,)),
         ],
         compiler_params=pltpu.CompilerParams(collective_id=0, has_side_effects=True, vmem_limit_bytes=60 << 20),
         name="collide",
     )(
-        g3.reshape(nb, KA, 2, 128), w3.reshape(nb, KA, 2, 128), hamilton, equal_time, quad_class, live_count,
+        g3.reshape(nb, KA, 2, 128), w3.reshape(nb, KA, 2, 128), hamilton, equal_time, quad_class, live_count.reshape(1, 1),
         jnp.asarray(phase_tables()), jnp.asarray(contract_table(), dtype=bf16),
     )
     stepped = pl.pallas_call(
         propagate_kernel,
         out_shape=jax.ShapeDtypeStruct((nb, tb, 128), f32),
-        in_specs=[vmem, hbm],
+        in_specs=[hbm, hbm],
         out_specs=hbm,
         scratch_shapes=[
+            pltpu.VMEM((24, 128), f32),
             pltpu.VMEM((nb, tb, 128), f32),
             pltpu.VMEM((nb, tb, 128), f32),
             pltpu.VMEM((16, 24, 128), f32),
-            pltpu.SemaphoreType.DMA((6,)),
+            pltpu.SemaphoreType.DMA((7,)),
         ],
         name="propagate",
     )(eff, g3)

time: 55 us -> 53.6 us (0.975)
  Pallas kernels: 54.1 us -> 52.8 us
    pallas_call x1, Pallas kernels: 50.9 us -> 50.2 us  [per_device(): pl.pallas_call(collide_kernel, out_shape=jax.ShapeDtypeStruct((24, 128),...]
    pallas_call x1, Pallas kernels: 3.25 us -> 2.57 us  [per_device(): pl.pallas_call(propagate_kernel, out_shape=jax.ShapeDtypeStruct((nb, tb,...]
where the time goes in v3:
time: 53.6 us; the launch traced here: 53.4 us
  Pallas kernels  52.8 us (99%)
  between operations  0.66 us (1%)
    pallas_call x1, Pallas kernels, per_device(): pl.pallas_call(collide_kernel, out_shape=jax.ShapeDtypeStruct((24, 128),...  50.2 us
    pallas_call x1, Pallas kernels, per_device(): pl.pallas_call(propagate_kernel, out_shape=jax.ShapeDtypeStruct((nb, tb,...  2.57 us

profile of v3, /device:TPU:2, one launch (start us, length us, event | category | flops | bytes accessed | tf_op | source)
XLA Modules:
  0.0 53.4 jit_solution(16317796885549979129)
XLA Ops:
  0.7 50.2 %collide.1.eff_in = f32[24,128]{1,0:T(8,128)} custom-call(f32[18,32,2,128]{3,2,1,0:T(2,128)} %bitcast.9, f32[18,32,2,128]{3,2,1,0:T(2,128)} %bitcast.11, f32[18,128]{1,0:T(8,128)} %ham_in.1, f32[18,128]{1,0:T(8,128)} %eq_in.1, s32[64]{0:T(128)} %qc_in.1, s32[1,1]{1,0:T(1,128)} %bitcast.8.lc_in, f32[2,4,24,288]{3,2,1,0:T(8,128)} %constant.4.clone.tab, ...), custom_call_target="tpu_custom_call" | custom-call | tf_op jit(solution)/shard_map/collide/pallas_call | solution.py:347
  50.9 2.6 %propagate.1 = f32[18,64,128]{2,1,0:T(8,128)} custom-call(f32[24,128]{1,0:T(8,128)} %collide.1.eff_in, f32[18,64,128]{2,1,0:T(8,128)} %bitcast.10), custom_call_target="tpu_custom_call" | custom-call | tf_op jit(solution)/shard_map/propagate/pallas_call | solution.py:383

commit v4 on v3

--- a/solution.py
+++ b/solution.py
@@ -258,7 +258,8 @@
                 v = s0 * gr[group, 2 * d] + s1 * gr[group, 2 * d + 1]
                 pr[n % 2, 0, rows, pl.ds(128 * d, 128)], pr[n % 2, 1, rows, pl.ds(128 * d, 128)] = split(v)
         at = pl.ds(pl.multiple_of(BLK * block(n), 16), BLK)
-        part[at, :] = (dot(pr[n % 2, 0], conv[...]) + dot(pr[n % 2, 1], conv[...])) + density
+        both = dot(pr[n % 2].reshape(2 * BLK, 2048), conv[...])
+        part[at, :] = (both[:BLK] + both[BLK:]) + density
         for d in range(8 if n < 3 else 7):
             to = block(n) * 8 + lax.rem(2 * y + c + 4 + d if n < 3 else 2 * y + c + 1 + d, 8)
             pltpu.make_async_remote_copy(
@@ -330,7 +331,8 @@
             mh, ml = split(jnp.concatenate(rows, axis=0))
             v = gv[k]
             vh, vl = split(v)
-            ov[k] = v + dot3(vh, vl, mh, ml)
+            both = dot(vh, jnp.concatenate([mh, ml], axis=1))
+            ov[k] = v + (both[:, :128] + (both[:, 128:] + dot(vl, mh)))
         copy = pltpu.make_async_copy(ov.at[pl.ds(per * i, per)], out.at[pl.ds(per * i, per)], sem.at[groups + i])
         copy.start()
         flush.append(copy)

time: 53.6 us -> 53.5 us (level)
  the two profiles are of different devices: /device:TPU:2 before, /device:TPU:6 now
where the time goes in v4:
time: 53.5 us; the launch traced here: 53.3 us
  Pallas kernels  52.7 us (99%)
  between operations  0.66 us (1%)
    pallas_call x1, Pallas kernels, per_device(): pl.pallas_call(collide_kernel, out_shape=jax.ShapeDtypeStruct((24, 128),...  50.2 us
    pallas_call x1, Pallas kernels, per_device(): pl.pallas_call(propagate_kernel, out_shape=jax.ShapeDtypeStruct((nb, tb,...  2.43 us

profile of v4, /device:TPU:6, one launch (start us, length us, event | category | flops | bytes accessed | tf_op | source)
XLA Modules:
  0.0 53.3 jit_solution(12446375109657414006)
XLA Ops:
  0.7 50.2 %collide.1.eff_in = f32[24,128]{1,0:T(8,128)} custom-call(f32[18,32,2,128]{3,2,1,0:T(2,128)} %bitcast.9, f32[18,32,2,128]{3,2,1,0:T(2,128)} %bitcast.11, f32[18,128]{1,0:T(8,128)} %ham_in.1, f32[18,128]{1,0:T(8,128)} %eq_in.1, s32[64]{0:T(128)} %qc_in.1, s32[1,1]{1,0:T(1,128)} %bitcast.8.lc_in, f32[2,4,24,288]{3,2,1,0:T(8,128)} %constant.4.clone.tab, ...), custom_call_target="tpu_custom_call" | custom-call | tf_op jit(solution)/shard_map/collide/pallas_call | solution.py:349
  50.9 2.4 %propagate.1 = f32[18,64,128]{2,1,0:T(8,128)} custom-call(f32[24,128]{1,0:T(8,128)} %collide.1.eff_in, f32[18,64,128]{2,1,0:T(8,128)} %bitcast.10), custom_call_target="tpu_custom_call" | custom-call | tf_op jit(solution)/shard_map/propagate/pallas_call | solution.py:385
